TPU v7x, 32 devices: a whole 2x2x4 slice. The times are simulated.
32 devices in a mesh: groups: 2 (over y), section: 4 (over z), head: 4 (over x, core).
Axes of the slice: x: 2, y: 2, z: 4, core: 2. Of those that a mesh axis runs over, the one named last changes fastest.
Arguments:
- queries: bfloat16 [1024, 2048], P(('groups', 'section'), 'head'), parts along dimension 0, may hold values from -16 to 16
- token_key_rows: bfloat16 [1024, 1024], P(('groups', 'section'), 'head'), parts along dimension 0, may hold values from -16 to 16
- token_value_rows: bfloat16 [1024, 1024], P(('groups', 'section'), 'head'), parts along dimension 0, may hold values from -6 to 6
- residual: bfloat16 [1024, 5376], P(('groups', 'section', 'head')), parts along dimension 0, may hold values from -6 to 6
- prefix: int32 [8], P('groups'), parts along dimension 0, may hold values from 0 to 128, as said below
- out_weight: bfloat16 [2048, 5376], P('head', 'section'), may hold values from -1 to 1
- post_gain: float32 [5376], replicated, may hold values from 0.25 to 1.75
Outputs:
- layer_out: bfloat16 [1024, 5376], P(('groups', 'section', 'head')), parts along dimension 0
There are 2 independent parts, one for each index of `groups`. A program takes and returns all parts, laid end to end along the dimension named above; an argument that names none is the same for every part. Nothing has to cross between parts.
Inputs may be any that keep to these rules, and one draw needn't show every extreme that they name: `prefix`: some section at index 1 or higher has the most, 128.
All inputs are finite; a program needn't handle non-finite values.
Results may differ from a plain program's by a relative error of at most 0.012.
Values may be sent and summed in bfloat16 or wider, within the bound.
A program may use at most 64 MiB of HBM per device.

v0:
```python
import jax
import jax.numpy as jnp
from jax import lax
from jax.sharding import PartitionSpec as P

HEAD_SIZE = 128


score_scale = 168.0 ** (-0.5)
floor_value = -1e30
norm_eps = 1e-06


def shifted(value, axis, steps):
    count = lax.axis_size(axis)
    leading, last = (max(0, -steps), min(count, count - steps))
    return lax.ppermute(value, axis, [(source, source + steps) for source in range(leading, last)])


def empty_state(row_count, key_heads, group_width):
    running_max = jnp.full((key_heads, group_width, row_count), floor_value, jnp.float32)
    running_sum = jnp.zeros((key_heads, group_width, row_count), jnp.float32)
    weighted = jnp.zeros((row_count, key_heads, group_width, HEAD_SIZE), jnp.float32)
    return (running_max, running_sum, weighted)


def attend(
    status, query_tile_block, query_pos, lower_pos, key_tile_block, value_tile_block, key_pos
):
    running_max, running_sum, weighted = status
    row_count = query_tile_block.shape[0]
    key_heads = key_tile_block.shape[1] // HEAD_SIZE
    group_width = query_tile_block.shape[1] // (key_heads * HEAD_SIZE)
    query_four = query_tile_block.reshape(row_count, key_heads, group_width, HEAD_SIZE)
    key_three = key_tile_block.reshape(key_tile_block.shape[0], key_heads, HEAD_SIZE)
    value_three = value_tile_block.reshape(value_tile_block.shape[0], key_heads, HEAD_SIZE)
    scores = (
        jnp.einsum("qkgd,pkd->kgqp", query_four, key_three, preferred_element_type=jnp.float32)
        * score_scale
    )
    visible = (key_pos[None, :] <= query_pos[:, None]) & (key_pos[None, :] >= lower_pos)
    masked = jnp.where(visible, scores, floor_value)
    new_max = jnp.maximum(running_max, jnp.max(masked, axis=-1))
    carry_scale = jnp.exp(running_max - new_max)
    weights = jnp.where(visible, jnp.exp(masked - new_max[..., None]), 0.0)
    running_sum = carry_scale * running_sum + jnp.sum(weights, axis=-1)
    product = jnp.einsum(
        "kgqp,pkd->qkgd",
        weights.astype(jnp.bfloat16),
        value_three,
        preferred_element_type=jnp.float32,
    )
    weighted = jnp.transpose(carry_scale, (2, 0, 1))[..., None] * weighted + product
    return (new_max, running_sum, weighted)


def local(queries, token_key_rows, token_value_rows, residual, prefix, out_weight, post_gain):
    row_count = queries.shape[0]
    key_heads = token_key_rows.shape[1] // HEAD_SIZE
    group_width = queries.shape[1] // (key_heads * HEAD_SIZE)
    section_total = lax.axis_size("section")
    section_index = lax.axis_index("section")
    reachable_blocks = 3 * section_total // 8
    base_rows = jnp.arange(row_count, dtype=jnp.int32)
    own_pos = section_index * row_count + base_rows
    seen_tokens = jnp.minimum(section_index * row_count, prefix[section_index])
    lower_pos = section_index * row_count - seen_tokens
    block_count = (seen_tokens + row_count - 1) // row_count
    blank = empty_state(row_count, key_heads, group_width)
    states = attend(blank, queries, own_pos, lower_pos, token_key_rows, token_value_rows, own_pos)

    def process(distance, key_tile_block, value_tile_block, mine):
        key_pos = (section_index - distance) * row_count + base_rows
        use_mine = distance <= block_count
        return lax.cond(
            use_mine,
            lambda current: attend(
                current, queries, own_pos, lower_pos, key_tile_block, value_tile_block, key_pos
            ),
            lambda current: current,
            mine,
        )

    held_keys = token_key_rows[None]
    held_values = token_value_rows[None]
    stride = 1
    while stride <= reachable_blocks:
        amount_moved = min(stride, reachable_blocks + 1 - stride)
        moved_keys, moved_values = shifted(
            (held_keys[:amount_moved], held_values[:amount_moved]), "section", stride
        )
        held_keys = jnp.concatenate([held_keys, moved_keys], axis=0)
        held_values = jnp.concatenate([held_values, moved_values], axis=0)
        stride = stride * 2

    def visit_block(distance, inner):
        key_tile_block = lax.dynamic_index_in_dim(held_keys, distance, 0, keepdims=False)
        value_tile_block = lax.dynamic_index_in_dim(held_values, distance, 0, keepdims=False)
        return process(distance, key_tile_block, value_tile_block, inner)

    states = lax.fori_loop(1, reachable_blocks + 1, visit_block, states)
    attention = states[2] / jnp.transpose(states[1], (2, 0, 1))[..., None]
    attention = attention.reshape(row_count, key_heads * group_width * HEAD_SIZE).astype(
        jnp.bfloat16
    )
    partial_out = jnp.dot(
        attention,
        lax.all_gather(out_weight, "section", axis=1, tiled=True),
        preferred_element_type=jnp.float32,
    )
    summed = lax.psum_scatter(
        partial_out.astype(jnp.bfloat16), "head", scatter_dimension=0, tiled=True
    ).astype(jnp.float32)
    mean_square = jnp.mean(summed * summed, axis=-1, keepdims=True)
    normed = summed * lax.rsqrt(mean_square + norm_eps) * post_gain[None, :]
    return (residual.astype(jnp.float32) + normed).astype(jnp.bfloat16)


def solution(mesh):
    placed = (
        P(("groups", "section"), "head"),
        P(("groups", "section"), "head"),
        P(("groups", "section"), "head"),
        P(("groups", "section", "head"), None),
        P("groups"),
        P("head", "section"),
        P(),
    )
    return jax.shard_map(
        local,
        mesh=mesh,
        in_specs=placed,
        out_specs=P(("groups", "section", "head"), None),
        check_vma=False,
    )
```

profile of v0, /device:TPU:0, one launch (start us, length us, event | category | flops | bytes accessed | tf_op | source)
XLA Modules:
  0.0 154.8 jit_solution(12587733265547962576)
XLA Ops:
  6.5 0.0 all-gather.2.cloned.1.call-start
  6.5 0.7 all-gather.2.cloned.1.call-update
  7.3 0.0 reduce-scatter.2.cloned.1.call-start
  7.3 5.0 %collective-permute-start.1 = (bf16[1,128,256]{2,1,0:T(8,128)(2,1)}, bf16[1,128,256]{2,1,0:T(8,128)(2,1)S(1)}, u32[]{:S(2)}, u32[]{:S(2)}) collective-permute-start(bf16[1,128,256]{2,1,0:T(8,128)(2,1)} %bitcast.34), channel_id=1, source_target_pairs={{0,4},{4,8},{8,12},{1,5},{5,9},{9,13},{2,6},{6,10},{10,14},{3,7},{... | collective-permute-start | bytes 196616 | tf_op jit(solution)/shard_map/ppermute | solution.py:17
  12.3 3.5 %collective-permute-start = (bf16[1,128,256]{2,1,0:T(8,128)(2,1)}, bf16[1,128,256]{2,1,0:T(8,128)(2,1)S(1)}, u32[]{:S(2)}, u32[]{:S(2)}) collective-permute-start(bf16[1,128,256]{2,1,0:T(8,128)(2,1)} %bitcast.35), channel_id=1, source_target_pairs={{0,4},{4,8},{8,12},{1,5},{5,9},{9,13},{2,6},{6,10},{10,14},{3,7},{... | collective-permute-start | bytes 196616 | tf_op jit(solution)/shard_map/ppermute | solution.py:17
  15.8 0.9 reshape.55
  16.6 0.9 reshape.57
  17.5 1.3 dynamic_slice.8
  19.5 1.0 reshape.56
  20.5 0.1 compare_and_fusion.1
  20.6 0.2 fusion.34
  20.8 0.1 fusion.22
  20.9 0.2 fusion.16
  21.2 0.0 collective-permute-done.1
  21.2 0.0 collective-permute-done
  21.2 0.0 copy-start
  21.2 0.0 copy-start.1
  21.3 0.2 conditional.1
  21.3 0.1 copy.39
  21.5 92.6 %all-gather.2.cloned.1.call-done = bf16[512,5376]{0,1:T(8,128)(2,1)} async-done(((bf16[512,1344]{0,1:T(8,128)(2,1)}), bf16[512,5376]{0,1:T(8,128)(2,1)}) %all-gather.2.cloned.1.call-update) | async-done | bytes 5505040 | tf_op jit(solution)/shard_map/all_gather | solution.py:108
  114.0 5.6 %convolution_convert_fusion = bf16[128,5376]{1,0:T(8,128)(2,1)} fusion(bf16[128,512]{0,1:T(8,128)(2,1)S(1)} %bitcast.31, bf16[512,5376]{0,1:T(8,128)(2,1)} %all-gather.2.cloned.1.call-done), kind=kOutput, calls=%fused_computation.21 | convolution fusion | flops 705331200 | bytes 7012352 | tf_op jit(solution)/shard_map/dot_general | solution.py:106
  119.6 0.0 reduce-scatter.2.cloned.1.call-update
  119.7 25.2 %reduce-scatter.2.cloned.1.call-done = bf16[32,5376]{1,0:T(8,128)(2,1)} async-done(((bf16[128,5376]{1,0:T(8,128)(2,1)}), bf16[32,5376]{1,0:T(8,128)(2,1)}) %reduce-scatter.2.cloned.1.call-update) | async-done | bytes 344080 | tf_op jit(solution)/shard_map/reduce_scatter | solution.py:111
  144.9 1.2 fusion.17
  146.1 0.0 copy-done
  146.1 0.0 copy-done.1
  146.1 1.9 %fusion.20 = bf16[32,5376]{1,0:T(8,128)(2,1)} fusion(bf16[32,5376]{1,0:T(8,128)(2,1)} %reduce-scatter.2.cloned.1.call-done, bf16[32,5376]{1,0:T(8,128)(2,1)S(1)} %copy-done, f32[5376]{0:T(1024)S(1)} %copy-done.1, f32[32]{0:T(128)S(1)} %add_rsqrt_fusion), kind=kLoop, calls=%fused_computation.32 | loop fusion | flops 1032192 | bytes 1053824 | tf_op jit(solution)/shard_map/convert_element_type | solution.py:116
  (7 shorter events, 0.1 us)
Async XLA Ops:
  6.5 107.5 %all-gather.2.cloned.1.call-start = ((), (), s32[]{:S(2)}) async-start(), calls=%async_computation.1 | async-start | bytes 6881280 | tf_op jit(solution)/shard_map/all_gather | solution.py:108
  7.3 137.6 %reduce-scatter.2.cloned.1.call-start = ((), (), s32[]{:S(2)}) async-start(), calls=%async_computation.2 | async-start | bytes 1720320 | tf_op jit(solution)/shard_map/reduce_scatter | solution.py:111
  7.3 13.9 %collective-permute-start.1 = (bf16[1,128,256]{2,1,0:T(8,128)(2,1)}, bf16[1,128,256]{2,1,0:T(8,128)(2,1)S(1)}, u32[]{:S(2)}, u32[]{:S(2)}) collective-permute-start(bf16[1,128,256]{2,1,0:T(8,128)(2,1)} %bitcast.34), channel_id=1, source_target_pairs={{0,4},{4,8},{8,12},{1,5},{5,9},{9,13},{2,6},{6,10},{10,14},{3,7},{... | collective-permute-start | bytes 196616 | tf_op jit(solution)/shard_map/ppermute | solution.py:17
  12.3 8.9 %collective-permute-start = (bf16[1,128,256]{2,1,0:T(8,128)(2,1)}, bf16[1,128,256]{2,1,0:T(8,128)(2,1)S(1)}, u32[]{:S(2)}, u32[]{:S(2)}) collective-permute-start(bf16[1,128,256]{2,1,0:T(8,128)(2,1)} %bitcast.35), channel_id=1, source_target_pairs={{0,4},{4,8},{8,12},{1,5},{5,9},{9,13},{2,6},{6,10},{10,14},{3,7},{... | collective-permute-start | bytes 196616 | tf_op jit(solution)/shard_map/ppermute | solution.py:17
  21.2 124.8 %copy-start = (bf16[32,5376]{1,0:T(8,128)(2,1)S(1)}, bf16[32,5376]{1,0:T(8,128)(2,1)}, u32[]{:S(2)}) copy-start(bf16[32,5376]{1,0:T(8,128)(2,1)} %param.12) | copy-start | bytes 1032196
  21.2 124.8 %copy-start.1 = (f32[5376]{0:T(1024)S(1)}, f32[5376]{0:T(1024)}, u32[]{:S(2)}) copy-start(f32[5376]{0:T(1024)} %param.15) | copy-start | bytes 64516
Sparse Core Ops, SparseCore 0:
  8.9 105.0 all-gather.1
  119.8 25.0 reduce-scatter.1
where the time goes:
time: 155 us
  waiting for transfers between devices  119 us (77%)
  between operations  14.3 us (9%)
  starting transfers between devices  8.49 us (5%)
  matrix products  6.07 us (4%)
  local copies, waits for them, and re-layouts  4.16 us (3%)
  other arithmetic  3.28 us (2%)
    all_gather x1, waiting for transfers between devices, local(): lax.all_gather(out_weight, 'section', axis=1, tiled=True)  92.6 us
    reduce_scatter x1, waiting for transfers between devices, local(): lax.psum_scatter(partial_out.astype(jnp.bfloat16), 'head', scatter_dimens...  25.2 us
    ppermute x2, starting transfers between devices, shifted(): lax.ppermute(value, axis, [(source, source + steps) for source in range(l...  8.45 us
    dot_general x1, matrix products, local(): jnp.dot(attention, lax.all_gather(out_weight, 'section', axis=1, tiled=Tr...  5.61 us
  transfers between devices with their start and end apart: 4, of which 2 were waited for; matrix products, arithmetic and copies ran while one was open for 3% of the time, Pallas kernels for 0%

commit v1 on v0

--- a/solution.py
+++ b/solution.py
@@ -1,6 +1,10 @@
+import functools
+
 import jax
 import jax.numpy as jnp
 from jax import lax
+from jax.experimental import pallas as pl
+from jax.experimental.pallas import tpu as pltpu
 from jax.sharding import PartitionSpec as P
 
 HEAD_SIZE = 128
@@ -9,6 +13,389 @@
 score_scale = 168.0 ** (-0.5)
 floor_value = -1e30
 norm_eps = 1e-06
+MESH = pl.DeviceIdType.MESH
+
+
+def visiting_order(n):
+    return [sorted(range(n), key=lambda t: (abs(t - s), t)) for s in range(n)]
+
+
+def fused_kernel(
+    n,
+    heads,
+    prefix_ref,
+    q_hbm,
+    k_hbm,
+    v_hbm,
+    res_hbm,
+    w_hbm,
+    gain_hbm,
+    out_ref,
+    q_v,
+    k_v,
+    v_v,
+    k_prev,
+    v_prev,
+    res_v,
+    w_v,
+    gain_v,
+    attn,
+    pair_send,
+    pair_recv,
+    mine,
+    far_send,
+    far_recv,
+    done_send,
+    done_recv,
+    load_sem,
+    kv_send_sem,
+    kv_recv_sem,
+    attn_send_sem,
+    attn_recv_sem,
+    pair_send_sem,
+    pair_recv_sem,
+    far_send_sem,
+    far_recv_sem,
+    done_send_sem,
+    done_recv_sem,
+):
+    s = lax.axis_index("section")
+    h = lax.axis_index("head")
+    rows = q_hbm.shape[0]
+    own_rows = rows // heads
+    half = heads // 2
+    core = lax.rem(h, 2)
+    partner = h + 1 - 2 * core
+    far = lax.rem(h + 2, heads)
+    key_heads = k_hbm.shape[1] // HEAD_SIZE
+    group_width = q_hbm.shape[1] // k_hbm.shape[1]
+
+    def remote(source, target, send_sem, recv_sem, where):
+        return pltpu.make_async_remote_copy(
+            src_ref=source,
+            dst_ref=target,
+            send_sem=send_sem,
+            recv_sem=recv_sem,
+            device_id=where,
+            device_id_type=MESH,
+        )
+
+    loads = [
+        pltpu.make_async_copy(source, target, load_sem.at[i])
+        for i, (source, target) in enumerate(
+            (
+                (q_hbm, q_v),
+                (k_hbm, k_v),
+                (v_hbm, v_v),
+                (w_hbm, w_v),
+                (res_hbm, res_v),
+                (gain_hbm, gain_v),
+            )
+        )
+    ]
+    for load in loads:
+        load.start()
+
+    barrier = pltpu.get_barrier_semaphore()
+    for step in range(1, n):
+        pl.semaphore_signal(
+            barrier, inc=1, device_id={"section": lax.rem(s + step, n)}, device_id_type=MESH
+        )
+    pl.semaphore_signal(barrier, inc=1, device_id={"head": partner}, device_id_type=MESH)
+    pl.semaphore_signal(barrier, inc=1, device_id={"head": far}, device_id_type=MESH)
+    pl.semaphore_wait(barrier, n + 1)
+
+    def kv_copies():
+        above = {"section": lax.rem(s + 1, n)}
+        return (
+            remote(k_hbm, k_prev, kv_send_sem.at[0], kv_recv_sem.at[0], above),
+            remote(v_hbm, v_prev, kv_send_sem.at[1], kv_recv_sem.at[1], above),
+        )
+
+    @pl.when(s + 1 < n)
+    def _():
+        for copy in kv_copies():
+            copy.start()
+
+    @pl.when(s == 0)
+    def _():
+        k_prev[...] = jnp.zeros_like(k_prev)
+        v_prev[...] = jnp.zeros_like(v_prev)
+
+    seen = jnp.minimum(s * rows, prefix_ref[s])
+    wide = group_width * rows
+    q_row = lax.rem(lax.broadcasted_iota(jnp.int32, (wide, rows), 0), rows)
+    k_col = lax.broadcasted_iota(jnp.int32, (wide, rows), 1)
+    own_seen = k_col <= q_row
+    prev_seen = k_col >= rows - seen
+
+    for load in loads[:3]:
+        load.wait()
+
+    def head_columns(ref, at):
+        return ref[:, at * HEAD_SIZE : (at + 1) * HEAD_SIZE]
+
+    def scores_of(query, key):
+        return (
+            lax.dot_general(
+                query, key, (((1,), (1,)), ((), ())), preferred_element_type=jnp.float32
+            )
+            * score_scale
+        )
+
+    queries = [
+        jnp.concatenate(
+            [head_columns(q_v, kh * group_width + g) for g in range(group_width)], axis=0
+        )
+        for kh in range(key_heads)
+    ]
+    own_scores = [
+        jnp.where(own_seen, scores_of(queries[kh], head_columns(k_v, kh)), floor_value)
+        for kh in range(key_heads)
+    ]
+
+    @pl.when(s > 0)
+    def _():
+        for copy in kv_copies():
+            copy.wait_recv()
+
+    for kh in range(key_heads):
+        own = own_scores[kh]
+        prev = jnp.where(
+            prev_seen, scores_of(queries[kh], head_columns(k_prev, kh)), floor_value
+        )
+        top = jnp.max(jnp.maximum(own, prev), axis=-1, keepdims=True)
+        own_probs = jnp.where(own_seen, jnp.exp(own - top), 0.0)
+        prev_probs = jnp.where(prev_seen, jnp.exp(prev - top), 0.0)
+        total = jnp.sum(own_probs + prev_probs, axis=-1, keepdims=True)
+        combined = jnp.dot(
+            own_probs.astype(jnp.bfloat16),
+            head_columns(v_v, kh),
+            preferred_element_type=jnp.float32,
+        ) + jnp.dot(
+            prev_probs.astype(jnp.bfloat16),
+            head_columns(v_prev, kh),
+            preferred_element_type=jnp.float32,
+        )
+        result = (combined / total).astype(jnp.bfloat16)
+        for g in range(group_width):
+            at = kh * group_width + g
+            attn[s, :, at * HEAD_SIZE : (at + 1) * HEAD_SIZE] = result[
+                g * rows : (g + 1) * rows
+            ]
+
+    def attn_copy(slot, block, target):
+        return remote(
+            attn.at[block],
+            attn.at[block],
+            attn_send_sem.at[slot],
+            attn_recv_sem.at[block],
+            {"section": target},
+        )
+
+    @pl.when(s + 1 < n)
+    def _():
+        attn_copy(0, s, s + 1).start()
+
+    @pl.when(s > 0)
+    def _():
+        attn_copy(n, s, s - 1).start()
+
+    table = visiting_order(n)
+
+    def visited(k):
+        block = table[0][k]
+        for i in range(1, n):
+            block = jnp.where(s == i, table[i][k], block)
+        return block
+
+    blocks = [s] + [visited(k) for k in range(1, n)]
+
+    def onward(block):
+        target = jnp.where(block < s, s + 1, s - 1)
+        return target, jnp.logical_and(target >= 0, target < n)
+
+    def pair_copy(k):
+        return remote(
+            pair_send.at[k],
+            pair_recv.at[k],
+            pair_send_sem.at[k],
+            pair_recv_sem.at[k],
+            {"head": partner},
+        )
+
+    def far_copy(k):
+        return remote(
+            far_send.at[k],
+            far_recv.at[k],
+            far_send_sem.at[k],
+            far_recv_sem.at[k],
+            {"head": far},
+        )
+
+    def done_copy(k):
+        return remote(
+            done_send.at[k],
+            done_recv.at[s],
+            done_send_sem.at[k],
+            done_recv_sem.at[s],
+            {"section": blocks[k]},
+        )
+
+    far_group = lax.rem(h // 2 + 1, half)
+    near_group = h // 2
+
+    def piece(block, group, side):
+        start = pl.multiple_of((group * 2 + side) * own_rows, own_rows)
+        return attn[block, pl.ds(start, own_rows), :]
+
+    def multiply(k):
+        block = blocks[k]
+        left = jnp.concatenate(
+            [
+                piece(block, far_group, 1 - core),
+                piece(block, near_group, 1 - core),
+                piece(block, far_group, core),
+                piece(block, near_group, core),
+            ],
+            axis=0,
+        )
+        product = jnp.dot(left, w_v[...], preferred_element_type=jnp.float32)
+        pair_send[k] = product[: 2 * own_rows].astype(jnp.bfloat16)
+        mine[k] = product[2 * own_rows :]
+        pair_copy(k).start()
+
+    def add_pair(k):
+        pair_copy(k).wait_recv()
+        far_send[k] = (
+            mine[k, :own_rows, :] + pair_recv[k, :own_rows, :].astype(jnp.float32)
+        ).astype(jnp.bfloat16)
+        far_copy(k).start()
+
+    def add_far(k):
+        far_copy(k).wait_recv()
+        value = (
+            mine[k, own_rows:, :]
+            + pair_recv[k, own_rows:, :].astype(jnp.float32)
+            + far_recv[k].astype(jnp.float32)
+        ).astype(jnp.bfloat16)
+        if k == 0:
+            done_recv[s] = value
+        else:
+            done_send[k] = value
+            done_copy(k).start()
+
+    for k in range(n):
+        if k == 0:
+            loads[3].wait()
+        else:
+            block = blocks[k]
+            target, valid = onward(block)
+            attn_copy(k, block, s).wait_recv()
+
+            @pl.when(valid)
+            def _(k=k, block=block, target=target):
+                attn_copy(k, block, target).start()
+
+        multiply(k)
+        if k > 0:
+            add_far(k - 1)
+        add_pair(k)
+    add_far(n - 1)
+
+    loads[4].wait()
+    loads[5].wait()
+    for k in range(1, n):
+        block = blocks[k]
+        remote(
+            done_send.at[k],
+            done_recv.at[block],
+            done_send_sem.at[k],
+            done_recv_sem.at[block],
+            {"section": block},
+        ).wait_recv()
+
+    width = w_hbm.shape[1]
+    squares = jnp.zeros((own_rows, 1), jnp.float32)
+    for i in range(n):
+        value = done_recv[i].astype(jnp.float32)
+        squares = squares + jnp.sum(value * value, axis=-1, keepdims=True)
+    scale = lax.rsqrt(squares / (n * width) + norm_eps)
+    for i in range(n):
+        columns = slice(i * width, (i + 1) * width)
+        normed = done_recv[i].astype(jnp.float32) * scale * gain_v[:, columns]
+        out_ref[:, columns] = (res_v[:, columns].astype(jnp.float32) + normed).astype(
+            out_ref.dtype
+        )
+
+    @pl.when(s + 1 < n)
+    def _():
+        for copy in kv_copies():
+            copy.wait_send()
+        attn_copy(0, s, s + 1).wait_send()
+
+    @pl.when(s > 0)
+    def _():
+        attn_copy(n, s, s - 1).wait_send()
+
+    for k in range(n):
+        pair_copy(k).wait_send()
+        far_copy(k).wait_send()
+        if k > 0:
+            done_copy(k).wait_send()
+            target, valid = onward(blocks[k])
+
+            @pl.when(valid)
+            def _(k=k, target=target):
+                attn_copy(k, blocks[k], target).wait_send()
+
+
+def fused_local(
+    n, heads, queries, token_key_rows, token_value_rows, residual, prefix, out_weight, post_gain
+):
+    rows = queries.shape[0]
+    own_rows = rows // heads
+    width = out_weight.shape[1]
+    low = jnp.bfloat16
+    anywhere = pl.BlockSpec(memory_space=pl.ANY)
+    dma = pltpu.SemaphoreType.DMA
+    gain = post_gain[None, :]
+    return pl.pallas_call(
+        functools.partial(fused_kernel, n, heads),
+        out_shape=jax.ShapeDtypeStruct(residual.shape, residual.dtype),
+        in_specs=[pl.BlockSpec(memory_space=pltpu.SMEM)] + [anywhere] * 6,
+        out_specs=pl.BlockSpec(memory_space=pltpu.VMEM),
+        scratch_shapes=[
+            pltpu.VMEM(queries.shape, low),
+            pltpu.VMEM(token_key_rows.shape, low),
+            pltpu.VMEM(token_value_rows.shape, low),
+            pltpu.VMEM(token_key_rows.shape, low),
+            pltpu.VMEM(token_value_rows.shape, low),
+            pltpu.VMEM(residual.shape, low),
+            pltpu.VMEM(out_weight.shape, low),
+            pltpu.VMEM(gain.shape, jnp.float32),
+            pltpu.VMEM((n,) + queries.shape, low),
+            pltpu.VMEM((n, 2 * own_rows, width), low),
+            pltpu.VMEM((n, 2 * own_rows, width), low),
+            pltpu.VMEM((n, 2 * own_rows, width), jnp.float32),
+            pltpu.VMEM((n, own_rows, width), low),
+            pltpu.VMEM((n, own_rows, width), low),
+            pltpu.VMEM((n, own_rows, width), low),
+            pltpu.VMEM((n, own_rows, width), low),
+            dma((6,)),
+            dma((2,)),
+            dma((2,)),
+            dma((n + 1,)),
+            dma((n,)),
+            dma((n,)),
+            dma((n,)),
+            dma((n,)),
+            dma((n,)),
+            dma((n,)),
+            dma((n,)),
+        ],
+        compiler_params=pltpu.CompilerParams(collective_id=0, has_side_effects=True),
+    )(prefix, queries, token_key_rows, token_value_rows, residual, out_weight, gain)
 
 
 def shifted(value, axis, steps):
@@ -126,8 +513,12 @@
         P("head", "section"),
         P(),
     )
+    n, heads = mesh.shape["section"], mesh.shape["head"]
+    body = local
+    if 3 * n // 8 == 1 and heads == 4:
+        body = functools.partial(fused_local, n, heads)
     return jax.shard_map(
-        local,
+        body,
         mesh=mesh,
         in_specs=placed,
         out_specs=P(("groups", "section", "head"), None),

time: 155 us -> 43.1 us (0.28)
  waiting for transfers between devices: 119 us -> 0 us
  Pallas kernels: 0 us -> 37.2 us
  between operations: 14.3 us -> 0.01 us
  starting transfers between devices: 8.49 us -> 0 us
  matrix products: 6.07 us -> 0 us
  other arithmetic: 3.28 us -> 0 us
    all_gather x1 -> x0, waiting for transfers between devices: 92.6 us -> none  [local(): lax.all_gather(out_weight, 'section', axis=1, tiled=True)]
    pallas_call x0 -> x1, Pallas kernels: none -> 37.2 us  [fused_local(): pl.pallas_call(functools.partial(fused_kernel, n, heads), out_shape=jax.S...]
    reduce_scatter x1 -> x0, waiting for transfers between devices: 25.2 us -> none  [local(): lax.psum_scatter(partial_out.astype(jnp.bfloat16), 'head', scatter_dimens...]
    ppermute x2 -> x0, starting transfers between devices: 8.45 us -> none  [shifted(): lax.ppermute(value, axis, [(source, source + steps) for source in range(l...]
    dot_general x3 -> x0, matrix products: 6.07 us -> none  [the longest x1 5.61 us: local(): jnp.dot(attention, lax.all_gather(out_weight, 'section', axis=1, tiled=Tr...]
    unnamed x4 -> x2, local copies, waits for them, and re-layouts: 0.01 us -> 4.25 us
    reshape x3 -> x0, local copies, waits for them, and re-layouts: 2.71 us -> none  [the longest x1 0.98 us: attend(): query_tile_block.reshape(row_count, key_heads, group_width, HEAD_SIZE)]
    convert_element_type x2 -> x0, other arithmetic: 1.93 us -> none  [the longest x1 1.9 us: local(): return (residual.astype(jnp.float32) + normed).astype(jnp.bfloat16)]
  transfers between devices with their start and end apart: 4 -> 0, of which waited for: 2 -> 0; matrix products, arithmetic and copies ran while one was open for 3% -> 0% of each run, Pallas kernels for 0% -> 0%
where the time goes in v1:
time: 43.1 us; the launch traced here: 42.9 us
  Pallas kernels  37.2 us (86%)
  local copies, waits for them, and re-layouts  5.61 us (13%)
    pallas_call x1, Pallas kernels, fused_local(): pl.pallas_call(functools.partial(fused_kernel, n, heads), out_shape=jax.S...  37.2 us
    unnamed x2, local copies, waits for them, and re-layouts  4.25 us
    broadcast_in_dim x1, local copies, waits for them, and re-layouts, fused_local(): gain = post_gain[None, :]  1.36 us

profile of v1, /device:TPU:0, one launch (start us, length us, event | category | flops | bytes accessed | tf_op | source)
XLA Modules:
  0.0 42.9 jit_solution(2029069310718609358)
XLA Ops:
  0.0 1.4 %broadcast_in_dim.3.gain_hbm = f32[1,5376]{1,0:T(1,128)} reshape(f32[5376]{0:T(1024)} %param.13) | data formatting | bytes 43008 | tf_op jit(solution)/shard_map/broadcast_in_dim | solution.py:362
  1.4 2.5 %copy.8.w_hbm = bf16[512,1344]{1,0:T(8,128)(2,1)} copy(bf16[512,1344]{0,1:T(8,128)(2,1)} %param.12) | data formatting | bytes 2752512 | tf_op args[5]
  3.9 37.2 %shard_map.73 = bf16[32,5376]{1,0:T(8,128)(2,1)} custom-call(s32[4]{0:T(128)} %prefix_ref.1, bf16[128,512]{1,0:T(8,128)(2,1)} %q_hbm.1, bf16[128,256]{1,0:T(8,128)(2,1)} %k_hbm.1, bf16[128,256]{1,0:T(8,128)(2,1)} %v_hbm.1, bf16[32,5376]{1,0:T(8,128)(2,1)} %res_hbm.1, bf16[512,1344]{1,0:T(8,128)(2,1)} %copy.8.w_hbm, f32[1,5376]{1,0:T(1,128)} %broadcast_in_dim.3.gain_hbm), custom_call_target="tpu_custom_call" | custom-call | tf_op jit(solution)/shard_map/pallas_call | solution.py:363
  41.1 1.7 %copy.10 = bf16[32,5376]{1,0:T(8,128)(2,1)} copy(bf16[32,5376]{1,0:T(8,128)(2,1)} %shard_map.73) | data formatting | bytes 688128

commit v2 on v1

--- a/solution.py
+++ b/solution.py
@@ -13,6 +13,8 @@
 score_scale = 168.0 ** (-0.5)
 floor_value = -1e30
 norm_eps = 1e-06
+LANES = 128
+CHUNKS = 2
 MESH = pl.DeviceIdType.MESH
 
 
@@ -23,22 +25,19 @@
 def fused_kernel(
     n,
     heads,
+    chunks,
     prefix_ref,
     q_hbm,
     k_hbm,
     v_hbm,
-    res_hbm,
     w_hbm,
-    gain_hbm,
-    out_ref,
+    done_recv,
     q_v,
     k_v,
     v_v,
     k_prev,
     v_prev,
-    res_v,
     w_v,
-    gain_v,
     attn,
     pair_send,
     pair_recv,
@@ -46,7 +45,6 @@
     far_send,
     far_recv,
     done_send,
-    done_recv,
     load_sem,
     kv_send_sem,
     kv_recv_sem,
@@ -69,6 +67,9 @@
     far = lax.rem(h + 2, heads)
     key_heads = k_hbm.shape[1] // HEAD_SIZE
     group_width = q_hbm.shape[1] // k_hbm.shape[1]
+    width = w_hbm.shape[0]
+    edges = [LANES * round(width * c / (chunks * LANES)) for c in range(chunks)] + [width]
+    spans = [slice(edges[c], edges[c + 1]) for c in range(chunks)]
 
     def remote(source, target, send_sem, recv_sem, where):
         return pltpu.make_async_remote_copy(
@@ -88,8 +89,6 @@
                 (k_hbm, k_v),
                 (v_hbm, v_v),
                 (w_hbm, w_v),
-                (res_hbm, res_v),
-                (gain_hbm, gain_v),
             )
         )
     ]
@@ -158,6 +157,15 @@
     def _():
         for copy in kv_copies():
             copy.wait_recv()
+
+    def attn_copy(slot, block, kh, target):
+        return remote(
+            attn.at[block, kh],
+            attn.at[block, kh],
+            attn_send_sem.at[slot, kh],
+            attn_recv_sem.at[block, kh],
+            {"section": target},
+        )
 
     for kh in range(key_heads):
         own = own_scores[kh]
@@ -179,27 +187,17 @@
         )
         result = (combined / total).astype(jnp.bfloat16)
         for g in range(group_width):
-            at = kh * group_width + g
-            attn[s, :, at * HEAD_SIZE : (at + 1) * HEAD_SIZE] = result[
+            attn[s, kh, :, g * HEAD_SIZE : (g + 1) * HEAD_SIZE] = result[
                 g * rows : (g + 1) * rows
             ]
 
-    def attn_copy(slot, block, target):
-        return remote(
-            attn.at[block],
-            attn.at[block],
-            attn_send_sem.at[slot],
-            attn_recv_sem.at[block],
-            {"section": target},
-        )
-
-    @pl.when(s + 1 < n)
-    def _():
-        attn_copy(0, s, s + 1).start()
-
-    @pl.when(s > 0)
-    def _():
-        attn_copy(n, s, s - 1).start()
+        @pl.when(s + 1 < n)
+        def _(kh=kh):
+            attn_copy(0, s, kh, s + 1).start()
+
+        @pl.when(s > 0)
+        def _(kh=kh):
+            attn_copy(n, s, kh, s - 1).start()
 
     table = visiting_order(n)
 
@@ -215,30 +213,30 @@
         target = jnp.where(block < s, s + 1, s - 1)
         return target, jnp.logical_and(target >= 0, target < n)
 
-    def pair_copy(k):
+    def pair_copy(k, c):
         return remote(
-            pair_send.at[k],
-            pair_recv.at[k],
-            pair_send_sem.at[k],
-            pair_recv_sem.at[k],
+            pair_send.at[k, :, spans[c]],
+            pair_recv.at[k, :, spans[c]],
+            pair_send_sem.at[k, c],
+            pair_recv_sem.at[k, c],
             {"head": partner},
         )
 
-    def far_copy(k):
+    def far_copy(k, c):
         return remote(
-            far_send.at[k],
-            far_recv.at[k],
-            far_send_sem.at[k],
-            far_recv_sem.at[k],
+            far_send.at[k, :, spans[c]],
+            far_recv.at[k, :, spans[c]],
+            far_send_sem.at[k, c],
+            far_recv_sem.at[k, c],
             {"head": far},
         )
 
-    def done_copy(k):
+    def done_copy(k, c):
         return remote(
-            done_send.at[k],
-            done_recv.at[s],
-            done_send_sem.at[k],
-            done_recv_sem.at[s],
+            done_send.at[k, :, spans[c]],
+            done_recv.at[s, :, spans[c]],
+            done_send_sem.at[k, c],
+            done_recv_sem.at[s, c],
             {"section": blocks[k]},
         )
 
@@ -247,7 +245,9 @@
 
     def piece(block, group, side):
         start = pl.multiple_of((group * 2 + side) * own_rows, own_rows)
-        return attn[block, pl.ds(start, own_rows), :]
+        return jnp.concatenate(
+            [attn[block, kh, pl.ds(start, own_rows), :] for kh in range(key_heads)], axis=1
+        )
 
     def multiply(k):
         block = blocks[k]
@@ -260,30 +260,40 @@
             ],
             axis=0,
         )
-        product = jnp.dot(left, w_v[...], preferred_element_type=jnp.float32)
-        pair_send[k] = product[: 2 * own_rows].astype(jnp.bfloat16)
-        mine[k] = product[2 * own_rows :]
-        pair_copy(k).start()
+        for c in range(chunks):
+            product = lax.dot_general(
+                left,
+                w_v[spans[c], :],
+                (((1,), (1,)), ((), ())),
+                preferred_element_type=jnp.float32,
+            )
+            pair_send[k, :, spans[c]] = product[: 2 * own_rows].astype(jnp.bfloat16)
+            mine[k, :, spans[c]] = product[2 * own_rows :]
+            pair_copy(k, c).start()
 
     def add_pair(k):
-        pair_copy(k).wait_recv()
-        far_send[k] = (
-            mine[k, :own_rows, :] + pair_recv[k, :own_rows, :].astype(jnp.float32)
-        ).astype(jnp.bfloat16)
-        far_copy(k).start()
+        for c in range(chunks):
+            span = spans[c]
+            pair_copy(k, c).wait_recv()
+            far_send[k, :, span] = (
+                mine[k, :own_rows, span] + pair_recv[k, :own_rows, span].astype(jnp.float32)
+            ).astype(jnp.bfloat16)
+            far_copy(k, c).start()
 
     def add_far(k):
-        far_copy(k).wait_recv()
-        value = (
-            mine[k, own_rows:, :]
-            + pair_recv[k, own_rows:, :].astype(jnp.float32)
-            + far_recv[k].astype(jnp.float32)
-        ).astype(jnp.bfloat16)
-        if k == 0:
-            done_recv[s] = value
-        else:
-            done_send[k] = value
-            done_copy(k).start()
+        for c in range(chunks):
+            span = spans[c]
+            far_copy(k, c).wait_recv()
+            value = (
+                mine[k, own_rows:, span]
+                + pair_recv[k, own_rows:, span].astype(jnp.float32)
+                + far_recv[k, :, span].astype(jnp.float32)
+            ).astype(jnp.bfloat16)
+            if k == 0:
+                done_recv[s, :, span] = value
+            else:
+                done_send[k, :, span] = value
+                done_copy(k, c).start()
 
     for k in range(n):
         if k == 0:
@@ -291,11 +301,12 @@
         else:
             block = blocks[k]
             target, valid = onward(block)
-            attn_copy(k, block, s).wait_recv()
-
-            @pl.when(valid)
-            def _(k=k, block=block, target=target):
-                attn_copy(k, block, target).start()
+            for kh in range(key_heads):
+                attn_copy(k, block, kh, s).wait_recv()
+
+                @pl.when(valid)
+                def _(k=k, kh=kh, block=block, target=target):
+                    attn_copy(k, block, kh, target).start()
 
         multiply(k)
         if k > 0:
@@ -303,51 +314,57 @@
         add_pair(k)
     add_far(n - 1)
 
-    loads[4].wait()
-    loads[5].wait()
     for k in range(1, n):
         block = blocks[k]
-        remote(
-            done_send.at[k],
-            done_recv.at[block],
-            done_send_sem.at[k],
-            done_recv_sem.at[block],
-            {"section": block},
-        ).wait_recv()
-
-    width = w_hbm.shape[1]
-    squares = jnp.zeros((own_rows, 1), jnp.float32)
+        for c in range(chunks):
+            remote(
+                done_send.at[k, :, spans[c]],
+                done_recv.at[block, :, spans[c]],
+                done_send_sem.at[k, c],
+                done_recv_sem.at[block, c],
+                {"section": block},
+            ).wait_recv()
+
+    @pl.when(s + 1 < n)
+    def _():
+        for copy in kv_copies():
+            copy.wait_send()
+        for kh in range(key_heads):
+            attn_copy(0, s, kh, s + 1).wait_send()
+
+    @pl.when(s > 0)
+    def _():
+        for kh in range(key_heads):
+            attn_copy(n, s, kh, s - 1).wait_send()
+
+    for k in range(n):
+        for c in range(chunks):
+            pair_copy(k, c).wait_send()
+            far_copy(k, c).wait_send()
+            if k > 0:
+                done_copy(k, c).wait_send()
+        if k > 0:
+            target, valid = onward(blocks[k])
+
+            @pl.when(valid)
+            def _(k=k, target=target):
+                for kh in range(key_heads):
+                    attn_copy(k, blocks[k], kh, target).wait_send()
+
+
+def norm_kernel(summed_ref, res_ref, gain_ref, out_ref):
+    n, _, width = summed_ref.shape
+    squares = 0.0
     for i in range(n):
-        value = done_recv[i].astype(jnp.float32)
+        value = summed_ref[i].astype(jnp.float32)
         squares = squares + jnp.sum(value * value, axis=-1, keepdims=True)
     scale = lax.rsqrt(squares / (n * width) + norm_eps)
     for i in range(n):
         columns = slice(i * width, (i + 1) * width)
-        normed = done_recv[i].astype(jnp.float32) * scale * gain_v[:, columns]
-        out_ref[:, columns] = (res_v[:, columns].astype(jnp.float32) + normed).astype(
+        normed = summed_ref[i].astype(jnp.float32) * scale * gain_ref[columns][None, :]
+        out_ref[:, columns] = (res_ref[:, columns].astype(jnp.float32) + normed).astype(
             out_ref.dtype
         )
-
-    @pl.when(s + 1 < n)
-    def _():
-        for copy in kv_copies():
-            copy.wait_send()
-        attn_copy(0, s, s + 1).wait_send()
-
-    @pl.when(s > 0)
-    def _():
-        attn_copy(n, s, s - 1).wait_send()
-
-    for k in range(n):
-        pair_copy(k).wait_send()
-        far_copy(k).wait_send()
-        if k > 0:
-            done_copy(k).wait_send()
-            target, valid = onward(blocks[k])
-
-            @pl.when(valid)
-            def _(k=k, target=target):
-                attn_copy(k, blocks[k], target).wait_send()
 
 
 def fused_local(
@@ -356,46 +373,51 @@
     rows = queries.shape[0]
     own_rows = rows // heads
     width = out_weight.shape[1]
+    key_heads = token_key_rows.shape[1] // HEAD_SIZE
     low = jnp.bfloat16
     anywhere = pl.BlockSpec(memory_space=pl.ANY)
+    vector = pl.BlockSpec(memory_space=pltpu.VMEM)
     dma = pltpu.SemaphoreType.DMA
-    gain = post_gain[None, :]
-    return pl.pallas_call(
-        functools.partial(fused_kernel, n, heads),
-        out_shape=jax.ShapeDtypeStruct(residual.shape, residual.dtype),
-        in_specs=[pl.BlockSpec(memory_space=pltpu.SMEM)] + [anywhere] * 6,
-        out_specs=pl.BlockSpec(memory_space=pltpu.VMEM),
+    weights = out_weight.T
+    summed = pl.pallas_call(
+        functools.partial(fused_kernel, n, heads, CHUNKS),
+        out_shape=jax.ShapeDtypeStruct((n, own_rows, width), low),
+        in_specs=[pl.BlockSpec(memory_space=pltpu.SMEM)] + [anywhere] * 4,
+        out_specs=vector,
         scratch_shapes=[
             pltpu.VMEM(queries.shape, low),
             pltpu.VMEM(token_key_rows.shape, low),
             pltpu.VMEM(token_value_rows.shape, low),
             pltpu.VMEM(token_key_rows.shape, low),
             pltpu.VMEM(token_value_rows.shape, low),
-            pltpu.VMEM(residual.shape, low),
-            pltpu.VMEM(out_weight.shape, low),
-            pltpu.VMEM(gain.shape, jnp.float32),
-            pltpu.VMEM((n,) + queries.shape, low),
+            pltpu.VMEM(weights.shape, low),
+            pltpu.VMEM((n, key_heads, rows, queries.shape[1] // key_heads), low),
             pltpu.VMEM((n, 2 * own_rows, width), low),
             pltpu.VMEM((n, 2 * own_rows, width), low),
             pltpu.VMEM((n, 2 * own_rows, width), jnp.float32),
             pltpu.VMEM((n, own_rows, width), low),
             pltpu.VMEM((n, own_rows, width), low),
             pltpu.VMEM((n, own_rows, width), low),
-            pltpu.VMEM((n, own_rows, width), low),
-            dma((6,)),
+            dma((4,)),
             dma((2,)),
             dma((2,)),
-            dma((n + 1,)),
-            dma((n,)),
-            dma((n,)),
-            dma((n,)),
-            dma((n,)),
-            dma((n,)),
-            dma((n,)),
-            dma((n,)),
+            dma((n + 1, key_heads)),
+            dma((n, key_heads)),
+            dma((n, CHUNKS)),
+            dma((n, CHUNKS)),
+            dma((n, CHUNKS)),
+            dma((n, CHUNKS)),
+            dma((n, CHUNKS)),
+            dma((n, CHUNKS)),
         ],
         compiler_params=pltpu.CompilerParams(collective_id=0, has_side_effects=True),
-    )(prefix, queries, token_key_rows, token_value_rows, residual, out_weight, gain)
+    )(prefix, queries, token_key_rows, token_value_rows, weights)
+    return pl.pallas_call(
+        norm_kernel,
+        out_shape=jax.ShapeDtypeStruct(residual.shape, residual.dtype),
+        in_specs=[vector] * 3,
+        out_specs=vector,
+    )(summed, residual, post_gain)
 
 
 def shifted(value, axis, steps):

time: 43.1 us -> 38.9 us (0.903)
  local copies, waits for them, and re-layouts: 5.61 us -> 0 us
  Pallas kernels: 37.2 us -> 38.7 us
    unnamed x2 -> x0, local copies, waits for them, and re-layouts: 4.25 us -> none
    pallas_call x1 -> x2, Pallas kernels: 37.2 us -> 38.7 us  [the longest x1 36.6 us: fused_local(): pl.pallas_call(functools.partial(fused_kernel, n, heads, CHUNKS), out_sha...]
    broadcast_in_dim x1 -> x0, local copies, waits for them, and re-layouts: 1.36 us -> none  [fused_local(): gain = post_gain[None, :]]
where the time goes in v2:
time: 38.9 us; the launch traced here: 38.7 us
  Pallas kernels  38.7 us (99%)
    pallas_call x1, Pallas kernels, fused_local(): pl.pallas_call(functools.partial(fused_kernel, n, heads, CHUNKS), out_sha...  36.6 us
    pallas_call x1, Pallas kernels, fused_local(): pl.pallas_call(norm_kernel, out_shape=jax.ShapeDtypeStruct(residual.shape...  2.17 us

profile of v2, /device:TPU:0, one launch (start us, length us, event | category | flops | bytes accessed | tf_op | source)
XLA Modules:
  0.0 38.7 jit_solution(9459529548797338814)
XLA Ops:
  0.0 36.6 %shard_map.73.summed_ref = bf16[4,32,1344]{2,1,0:T(8,128)(2,1)} custom-call(s32[4]{0:T(128)} %prefix_ref.1, bf16[128,512]{1,0:T(8,128)(2,1)} %q_hbm.1, bf16[128,256]{1,0:T(8,128)(2,1)} %k_hbm.1, bf16[128,256]{1,0:T(8,128)(2,1)} %v_hbm.1, bf16[1344,512]{1,0:T(8,128)(2,1)} %bitcast.1), custom_call_target="tpu_custom_call" | custom-call | tf_op jit(solution)/shard_map/pallas_call | solution.py:382
  36.6 2.2 %shard_map.74 = bf16[32,5376]{1,0:T(8,128)(2,1)} custom-call(bf16[4,32,1344]{2,1,0:T(8,128)(2,1)} %shard_map.73.summed_ref, bf16[32,5376]{1,0:T(8,128)(2,1)} %res_ref.1, f32[5376]{0:T(1024)} %gain_ref.1), custom_call_target="tpu_custom_call" | custom-call | tf_op jit(solution)/shard_map/pallas_call | solution.py:415

commit v3 on v2

--- a/solution.py
+++ b/solution.py
@@ -15,23 +15,41 @@
 norm_eps = 1e-06
 LANES = 128
 CHUNKS = 2
+VMEM_LIMIT = (60 * 1024 - 720) * 1024
 MESH = pl.DeviceIdType.MESH
 
 
 def visiting_order(n):
     return [sorted(range(n), key=lambda t: (abs(t - s), t)) for s in range(n)]
+
+
+def plan_of(s, n):
+    order = visiting_order(n)[s]
+    groups = [
+        [k for k in range(n) if abs(order[k] - s) == distance] for distance in range(n)
+    ]
+    plan, before = [], []
+    for group in filter(None, groups):
+        plan += [("take", k) for k in group if k]
+        plan += [("multiply", k) for k in group]
+        plan += [("pair", k) for k in group]
+        plan += [("far", k) for k in before]
+        before = group
+    plan += [("far", k) for k in before]
+    return tuple(plan)
 
 
 def fused_kernel(
     n,
     heads,
     chunks,
-    prefix_ref,
+    prefix_hbm,
     q_hbm,
     k_hbm,
     v_hbm,
     w_hbm,
     done_recv,
+    prefix_ref,
     q_v,
     k_v,
     v_v,
@@ -89,6 +107,7 @@
                 (k_hbm, k_v),
                 (v_hbm, v_v),
                 (w_hbm, w_v),
+                (prefix_hbm, prefix_ref),
             )
         )
     ]
@@ -104,23 +123,35 @@
     pl.semaphore_signal(barrier, inc=1, device_id={"head": far}, device_id_type=MESH)
     pl.semaphore_wait(barrier, n + 1)
 
-    def kv_copies():
+    def head_span(at):
+        return slice(at * HEAD_SIZE, (at + 1) * HEAD_SIZE)
+
+    def kv_copies(kh):
         above = {"section": lax.rem(s + 1, n)}
-        return (
-            remote(k_hbm, k_prev, kv_send_sem.at[0], kv_recv_sem.at[0], above),
-            remote(v_hbm, v_prev, kv_send_sem.at[1], kv_recv_sem.at[1], above),
-        )
+        span = head_span(kh)
+        return [
+            remote(
+                source.at[:, span],
+                target.at[:, span],
+                kv_send_sem.at[kh, i],
+                kv_recv_sem.at[kh, i],
+                above,
+            )
+            for i, (source, target) in enumerate(((k_hbm, k_prev), (v_hbm, v_prev)))
+        ]
 
     @pl.when(s + 1 < n)
     def _():
-        for copy in kv_copies():
-            copy.start()
+        for kh in range(key_heads):
+            for copy in kv_copies(kh):
+                copy.start()
 
     @pl.when(s == 0)
     def _():
         k_prev[...] = jnp.zeros_like(k_prev)
         v_prev[...] = jnp.zeros_like(v_prev)
 
+    loads[4].wait()
     seen = jnp.minimum(s * rows, prefix_ref[s])
     wide = group_width * rows
     q_row = lax.rem(lax.broadcasted_iota(jnp.int32, (wide, rows), 0), rows)
@@ -132,7 +163,7 @@
         load.wait()
 
     def head_columns(ref, at):
-        return ref[:, at * HEAD_SIZE : (at + 1) * HEAD_SIZE]
+        return ref[:, head_span(at)]
 
     def scores_of(query, key):
         return (
@@ -152,11 +183,6 @@
         jnp.where(own_seen, scores_of(queries[kh], head_columns(k_v, kh)), floor_value)
         for kh in range(key_heads)
     ]
-
-    @pl.when(s > 0)
-    def _():
-        for copy in kv_copies():
-            copy.wait_recv()
 
     def attn_copy(slot, block, kh, target):
         return remote(
@@ -168,6 +194,12 @@
         )
 
     for kh in range(key_heads):
+
+        @pl.when(s > 0)
+        def _(kh=kh):
+            for copy in kv_copies(kh):
+                copy.wait_recv()
+
         own = own_scores[kh]
         prev = jnp.where(
             prev_seen, scores_of(queries[kh], head_columns(k_prev, kh)), floor_value
@@ -295,24 +327,30 @@
                 done_send[k, :, span] = value
                 done_copy(k, c).start()
 
-    for k in range(n):
-        if k == 0:
-            loads[3].wait()
-        else:
-            block = blocks[k]
-            target, valid = onward(block)
-            for kh in range(key_heads):
-                attn_copy(k, block, kh, s).wait_recv()
-
-                @pl.when(valid)
-                def _(k=k, kh=kh, block=block, target=target):
-                    attn_copy(k, block, kh, target).start()
-
-        multiply(k)
-        if k > 0:
-            add_far(k - 1)
-        add_pair(k)
-    add_far(n - 1)
+    def pass_on(k):
+        block = blocks[k]
+        target, valid = onward(block)
+        for kh in range(key_heads):
+            attn_copy(k, block, kh, s).wait_recv()
+
+            @pl.when(valid)
+            def _(kh=kh):
+                attn_copy(k, block, kh, target).start()
+
+    actions = {"take": pass_on, "multiply": multiply, "pair": add_pair, "far": add_far}
+    loads[3].wait()
+    plans = {}
+    for i in range(n):
+        plans.setdefault(plan_of(i, n), []).append(i)
+    for plan, places in plans.items():
+        chosen = s == places[0]
+        for place in places[1:]:
+            chosen = jnp.logical_or(chosen, s == place)
+
+        @pl.when(chosen)
+        def _(plan=plan):
+            for name, k in plan:
+                actions[name](k)
 
     for k in range(1, n):
         block = blocks[k]
@@ -327,8 +365,9 @@
 
     @pl.when(s + 1 < n)
     def _():
-        for copy in kv_copies():
-            copy.wait_send()
+        for kh in range(key_heads):
+            for copy in kv_copies(kh):
+                copy.wait_send()
         for kh in range(key_heads):
             attn_copy(0, s, kh, s + 1).wait_send()
 
@@ -375,16 +414,17 @@
     width = out_weight.shape[1]
     key_heads = token_key_rows.shape[1] // HEAD_SIZE
     low = jnp.bfloat16
-    anywhere = pl.BlockSpec(memory_space=pl.ANY)
+    stays = pl.BlockSpec(memory_space=pltpu.HBM)
     vector = pl.BlockSpec(memory_space=pltpu.VMEM)
     dma = pltpu.SemaphoreType.DMA
     weights = out_weight.T
     summed = pl.pallas_call(
         functools.partial(fused_kernel, n, heads, CHUNKS),
         out_shape=jax.ShapeDtypeStruct((n, own_rows, width), low),
-        in_specs=[pl.BlockSpec(memory_space=pltpu.SMEM)] + [anywhere] * 4,
+        in_specs=[stays] * 5,
         out_specs=vector,
         scratch_shapes=[
+            pltpu.SMEM(prefix.shape, jnp.int32),
             pltpu.VMEM(queries.shape, low),
             pltpu.VMEM(token_key_rows.shape, low),
             pltpu.VMEM(token_value_rows.shape, low),
@@ -398,9 +438,9 @@
             pltpu.VMEM((n, own_rows, width), low),
             pltpu.VMEM((n, own_rows, width), low),
             pltpu.VMEM((n, own_rows, width), low),
-            dma((4,)),
-            dma((2,)),
-            dma((2,)),
+            dma((5,)),
+            dma((key_heads, 2)),
+            dma((key_heads, 2)),
             dma((n + 1, key_heads)),
             dma((n, key_heads)),
             dma((n, CHUNKS)),
@@ -410,13 +450,16 @@
             dma((n, CHUNKS)),
             dma((n, CHUNKS)),
         ],
-        compiler_params=pltpu.CompilerParams(collective_id=0, has_side_effects=True),
+        compiler_params=pltpu.CompilerParams(
+            collective_id=0, has_side_effects=True, vmem_limit_bytes=VMEM_LIMIT
+        ),
     )(prefix, queries, token_key_rows, token_value_rows, weights)
     return pl.pallas_call(
         norm_kernel,
         out_shape=jax.ShapeDtypeStruct(residual.shape, residual.dtype),
         in_specs=[vector] * 3,
         out_specs=vector,
+        compiler_params=pltpu.CompilerParams(vmem_limit_bytes=16 * 2**20),
     )(summed, residual, post_gain)
 
 

time: 38.9 us -> 34.7 us (0.89)
  Pallas kernels: 38.7 us -> 33.6 us
  local copies, waits for them, and re-layouts: 0 us -> 0.98 us
    pallas_call x1, Pallas kernels: 36.6 us -> 32.5 us  [fused_local(): pl.pallas_call(functools.partial(fused_kernel, n, heads, CHUNKS), out_sha...]
    pallas_call x1, Pallas kernels: 2.17 us -> 1.08 us  [fused_local(): pl.pallas_call(norm_kernel, out_shape=jax.ShapeDtypeStruct(residual.shape...]
    unnamed x0 -> x6, local copies, waits for them, and re-layouts: none -> 0.98 us
where the time goes in v3:
time: 34.7 us; the launch traced here: 34.6 us
  Pallas kernels  33.6 us (97%)
  local copies, waits for them, and re-layouts  0.98 us (3%)
    pallas_call x1, Pallas kernels, fused_local(): pl.pallas_call(functools.partial(fused_kernel, n, heads, CHUNKS), out_sha...  32.5 us
    pallas_call x1, Pallas kernels, fused_local(): pl.pallas_call(norm_kernel, out_shape=jax.ShapeDtypeStruct(residual.shape...  1.08 us
    unnamed x6, local copies, waits for them, and re-layouts  0.98 us

profile of v3, /device:TPU:0, one launch (start us, length us, event | category | flops | bytes accessed | tf_op | source)
XLA Modules:
  0.0 34.6 jit_solution(18061916937119791365)
XLA Ops:
  0.0 0.0 copy-start.2
  0.0 0.0 copy-start.1
  0.0 32.5 %shard_map.73.summed_ref = bf16[4,32,1344]{2,1,0:T(8,128)(2,1)} custom-call(s32[4]{0:T(128)} %prefix_hbm.1, bf16[128,512]{1,0:T(8,128)(2,1)} %q_hbm.1, bf16[128,256]{1,0:T(8,128)(2,1)} %k_hbm.1, bf16[128,256]{1,0:T(8,128)(2,1)} %v_hbm.1, bf16[1344,512]{1,0:T(8,128)(2,1)} %bitcast.1), custom_call_target="tpu_custom_call" | custom-call | tf_op jit(solution)/shard_map/pallas_call | solution.py:421
  32.5 0.0 copy-done.2
  32.5 0.0 copy-done.1
  32.5 0.0 copy-start
  32.5 1.0 %copy-done = bf16[4,32,1344]{2,1,0:T(8,128)(2,1)S(1)} copy-done((bf16[4,32,1344]{2,1,0:T(8,128)(2,1)S(1)}, bf16[4,32,1344]{2,1,0:T(8,128)(2,1)}, u32[]{:S(2)}) %copy-start) | copy-done | bytes 344088
  33.5 1.1 %shard_map.74 = bf16[32,5376]{1,0:T(8,128)(2,1)} custom-call(bf16[4,32,1344]{2,1,0:T(8,128)(2,1)S(1)} %copy-done, bf16[32,5376]{1,0:T(8,128)(2,1)S(1)} %copy-done.1, f32[5376]{0:T(1024)S(1)} %copy-done.2), custom_call_target="tpu_custom_call" | custom-call | tf_op jit(solution)/shard_map/pallas_call | solution.py:457
Async XLA Ops:
  0.0 32.5 %copy-start.2 = (f32[5376]{0:T(1024)S(1)}, f32[5376]{0:T(1024)}, u32[]{:S(2)}) copy-start(f32[5376]{0:T(1024)} %gain_ref.1) | copy-start | bytes 64516
  0.0 32.5 %copy-start.1 = (bf16[32,5376]{1,0:T(8,128)(2,1)S(1)}, bf16[32,5376]{1,0:T(8,128)(2,1)}, u32[]{:S(2)}) copy-start(bf16[32,5376]{1,0:T(8,128)(2,1)} %res_ref.1) | copy-start | bytes 1032196
  32.5 1.0 %copy-start = (bf16[4,32,1344]{2,1,0:T(8,128)(2,1)S(1)}, bf16[4,32,1344]{2,1,0:T(8,128)(2,1)}, u32[]{:S(2)}) copy-start(bf16[4,32,1344]{2,1,0:T(8,128)(2,1)} %shard_map.73.summed_ref) | copy-start | bytes 1032196

commit v4 on v3

--- a/solution.py
+++ b/solution.py
@@ -15,6 +15,7 @@
 norm_eps = 1e-06
 LANES = 128
 CHUNKS = 2
+ROW_PARTS = 1
 VMEM_LIMIT = (60 * 1024 - 720) * 1024
 MESH = pl.DeviceIdType.MESH
 
@@ -179,17 +180,30 @@
         )
         for kh in range(key_heads)
     ]
-    own_scores = [
-        jnp.where(own_seen, scores_of(queries[kh], head_columns(k_v, kh)), floor_value)
-        for kh in range(key_heads)
-    ]
-
-    def attn_copy(slot, block, kh, target):
+    own_parts = []
+    for kh in range(key_heads):
+        own = jnp.where(own_seen, scores_of(queries[kh], head_columns(k_v, kh)), floor_value)
+        own_top = jnp.max(own, axis=-1, keepdims=True)
+        own_probs = jnp.where(own_seen, jnp.exp(own - own_top), 0.0)
+        own_total = jnp.sum(own_probs, axis=-1, keepdims=True)
+        own_combined = jnp.dot(
+            own_probs.astype(jnp.bfloat16),
+            head_columns(v_v, kh),
+            preferred_element_type=jnp.float32,
+        )
+        own_parts.append((own_top, own_total, own_combined))
+
+    parts = [(kh, r) for kh in range(key_heads) for r in range(ROW_PARTS)]
+    part_rows = rows // ROW_PARTS
+
+    def attn_copy(slot, block, part, target):
+        kh, r = parts[part]
+        here = attn.at[block, kh, r * part_rows : (r + 1) * part_rows]
         return remote(
-            attn.at[block, kh],
-            attn.at[block, kh],
-            attn_send_sem.at[slot, kh],
-            attn_recv_sem.at[block, kh],
+            here,
+            here,
+            attn_send_sem.at[slot, part],
+            attn_recv_sem.at[block, part],
             {"section": target},
         )
 
@@ -200,19 +214,15 @@
             for copy in kv_copies(kh):
                 copy.wait_recv()
 
-        own = own_scores[kh]
+        own_top, own_total, own_combined = own_parts[kh]
         prev = jnp.where(
             prev_seen, scores_of(queries[kh], head_columns(k_prev, kh)), floor_value
         )
-        top = jnp.max(jnp.maximum(own, prev), axis=-1, keepdims=True)
-        own_probs = jnp.where(own_seen, jnp.exp(own - top), 0.0)
+        top = jnp.maximum(own_top, jnp.max(prev, axis=-1, keepdims=True))
         prev_probs = jnp.where(prev_seen, jnp.exp(prev - top), 0.0)
-        total = jnp.sum(own_probs + prev_probs, axis=-1, keepdims=True)
-        combined = jnp.dot(
-            own_probs.astype(jnp.bfloat16),
-            head_columns(v_v, kh),
-            preferred_element_type=jnp.float32,
-        ) + jnp.dot(
+        carry = jnp.exp(own_top - top)
+        total = carry * own_total + jnp.sum(prev_probs, axis=-1, keepdims=True)
+        combined = carry * own_combined + jnp.dot(
             prev_probs.astype(jnp.bfloat16),
             head_columns(v_prev, kh),
             preferred_element_type=jnp.float32,
@@ -223,13 +233,17 @@
                 g * rows : (g + 1) * rows
             ]
 
+        ready = [part for part in range(len(parts)) if parts[part][0] == kh]
+
+        @pl.when(s > 0)
+        def _(ready=ready):
+            for part in ready:
+                attn_copy(n, s, part, s - 1).start()
+
         @pl.when(s + 1 < n)
-        def _(kh=kh):
-            attn_copy(0, s, kh, s + 1).start()
-
-        @pl.when(s > 0)
-        def _(kh=kh):
-            attn_copy(n, s, kh, s - 1).start()
+        def _(ready=ready):
+            for part in ready:
+                attn_copy(0, s, part, s + 1).start()
 
     table = visiting_order(n)
 
@@ -270,6 +284,11 @@
             done_send_sem.at[k, c],
             done_recv_sem.at[s, c],
             {"section": blocks[k]},
+        )
+
+    def keep_copy(c):
+        return pltpu.make_async_copy(
+            done_send.at[0, :, spans[c]], done_recv.at[s, :, spans[c]], done_send_sem.at[0, c]
         )
 
     far_group = lax.rem(h // 2 + 1, half)
@@ -321,21 +340,21 @@
                 + pair_recv[k, own_rows:, span].astype(jnp.float32)
                 + far_recv[k, :, span].astype(jnp.float32)
             ).astype(jnp.bfloat16)
+            done_send[k, :, span] = value
             if k == 0:
-                done_recv[s, :, span] = value
+                keep_copy(c).start()
             else:
-                done_send[k, :, span] = value
                 done_copy(k, c).start()
 
     def pass_on(k):
         block = blocks[k]
         target, valid = onward(block)
-        for kh in range(key_heads):
-            attn_copy(k, block, kh, s).wait_recv()
+        for part in range(len(parts)):
+            attn_copy(k, block, part, s).wait_recv()
 
             @pl.when(valid)
-            def _(kh=kh):
-                attn_copy(k, block, kh, target).start()
+            def _(part=part):
+                attn_copy(k, block, part, target).start()
 
     actions = {"take": pass_on, "multiply": multiply, "pair": add_pair, "far": add_far}
     loads[3].wait()
@@ -368,13 +387,13 @@
         for kh in range(key_heads):
             for copy in kv_copies(kh):
                 copy.wait_send()
-        for kh in range(key_heads):
-            attn_copy(0, s, kh, s + 1).wait_send()
+        for part in range(len(parts)):
+            attn_copy(0, s, part, s + 1).wait_send()
 
     @pl.when(s > 0)
     def _():
-        for kh in range(key_heads):
-            attn_copy(n, s, kh, s - 1).wait_send()
+        for part in range(len(parts)):
+            attn_copy(n, s, part, s - 1).wait_send()
 
     for k in range(n):
         for c in range(chunks):
@@ -382,13 +401,15 @@
             far_copy(k, c).wait_send()
             if k > 0:
                 done_copy(k, c).wait_send()
+            else:
+                keep_copy(c).wait()
         if k > 0:
             target, valid = onward(blocks[k])
 
             @pl.when(valid)
             def _(k=k, target=target):
-                for kh in range(key_heads):
-                    attn_copy(k, blocks[k], kh, target).wait_send()
+                for part in range(len(parts)):
+                    attn_copy(k, blocks[k], part, target).wait_send()
 
 
 def norm_kernel(summed_ref, res_ref, gain_ref, out_ref):
@@ -422,7 +443,7 @@
         functools.partial(fused_kernel, n, heads, CHUNKS),
         out_shape=jax.ShapeDtypeStruct((n, own_rows, width), low),
         in_specs=[stays] * 5,
-        out_specs=vector,
+        out_specs=stays,
         scratch_shapes=[
             pltpu.SMEM(prefix.shape, jnp.int32),
             pltpu.VMEM(queries.shape, low),
@@ -441,8 +462,8 @@
             dma((5,)),
             dma((key_heads, 2)),
             dma((key_heads, 2)),
-            dma((n + 1, key_heads)),
-            dma((n, key_heads)),
+            dma((n + 1, key_heads * ROW_PARTS)),
+            dma((n, key_heads * ROW_PARTS)),
             dma((n, CHUNKS)),
             dma((n, CHUNKS)),
             dma((n, CHUNKS)),

time: 34.7 us -> 34.1 us (0.983)
  Pallas kernels: 33.6 us -> 32.9 us
    pallas_call x1, Pallas kernels: 32.5 us -> 31.9 us  [fused_local(): pl.pallas_call(functools.partial(fused_kernel, n, heads, CHUNKS), out_sha...]
where the time goes in v4:
time: 34.1 us; the launch traced here: 34 us
  Pallas kernels  32.9 us (96%)
  local copies, waits for them, and re-layouts  0.98 us (3%)
    pallas_call x1, Pallas kernels, fused_local(): pl.pallas_call(functools.partial(fused_kernel, n, heads, CHUNKS), out_sha...  31.9 us
    pallas_call x1, Pallas kernels, fused_local(): pl.pallas_call(norm_kernel, out_shape=jax.ShapeDtypeStruct(residual.shape...  1.08 us
    unnamed x6, local copies, waits for them, and re-layouts  0.98 us

profile of v4, /device:TPU:0, one launch (start us, length us, event | category | flops | bytes accessed | tf_op | source)
XLA Modules:
  0.0 34.0 jit_solution(4973922781912245158)
XLA Ops:
  0.0 0.0 copy-start.2
  0.0 0.0 copy-start.1
  0.0 31.9 %shard_map.73.summed_ref = bf16[4,32,1344]{2,1,0:T(8,128)(2,1)} custom-call(s32[4]{0:T(128)} %prefix_hbm.1, bf16[128,512]{1,0:T(8,128)(2,1)} %q_hbm.1, bf16[128,256]{1,0:T(8,128)(2,1)} %k_hbm.1, bf16[128,256]{1,0:T(8,128)(2,1)} %v_hbm.1, bf16[1344,512]{1,0:T(8,128)(2,1)} %bitcast.1), custom_call_target="tpu_custom_call" | custom-call | tf_op jit(solution)/shard_map/pallas_call | solution.py:442
  31.9 0.0 copy-done.2
  31.9 0.0 copy-done.1
  31.9 0.0 copy-start
  31.9 1.0 %copy-done = bf16[4,32,1344]{2,1,0:T(8,128)(2,1)S(1)} copy-done((bf16[4,32,1344]{2,1,0:T(8,128)(2,1)S(1)}, bf16[4,32,1344]{2,1,0:T(8,128)(2,1)}, u32[]{:S(2)}) %copy-start) | copy-done | bytes 344088
  32.9 1.1 %shard_map.74 = bf16[32,5376]{1,0:T(8,128)(2,1)} custom-call(bf16[4,32,1344]{2,1,0:T(8,128)(2,1)S(1)} %copy-done, bf16[32,5376]{1,0:T(8,128)(2,1)S(1)} %copy-done.1, f32[5376]{0:T(1024)S(1)} %copy-done.2), custom_call_target="tpu_custom_call" | custom-call | tf_op jit(solution)/shard_map/pallas_call | solution.py:478
Async XLA Ops:
  0.0 31.9 %copy-start.2 = (f32[5376]{0:T(1024)S(1)}, f32[5376]{0:T(1024)}, u32[]{:S(2)}) copy-start(f32[5376]{0:T(1024)} %gain_ref.1) | copy-start | bytes 64516
  0.0 31.9 %copy-start.1 = (bf16[32,5376]{1,0:T(8,128)(2,1)S(1)}, bf16[32,5376]{1,0:T(8,128)(2,1)}, u32[]{:S(2)}) copy-start(bf16[32,5376]{1,0:T(8,128)(2,1)} %res_ref.1) | copy-start | bytes 1032196
  31.9 1.0 %copy-start = (bf16[4,32,1344]{2,1,0:T(8,128)(2,1)S(1)}, bf16[4,32,1344]{2,1,0:T(8,128)(2,1)}, u32[]{:S(2)}) copy-start(bf16[4,32,1344]{2,1,0:T(8,128)(2,1)} %shard_map.73.summed_ref) | copy-start | bytes 1032196
